TPU v7x, 256 devices: a whole 4x4x8 slice. The times are simulated.
256 devices in a mesh: sx: 8 (over z_hi, x), sy: 4 (over z_lo), af: 8 (over y, core).
Axes of the slice: x: 4, y: 4, z: 8 (z_hi: 2, z_lo: 4; z = z_hi * 4 + z_lo), core: 2. Of those that a mesh axis runs over, the one named last changes fastest.
Arguments:
- volume: bfloat16 [8, 48, 48, 48, 128], P('af', 'sx', 'sy'), may hold values from -6 to 6
- kernel: bfloat16 [3, 3, 3, 128, 256], P(None, None, None, 'sx', ('sy', 'af')), may hold values from -0.109375 to 0.109375
- cotangent: bfloat16 [8, 256, 24, 576], P('sx', ('sy', 'af')), may hold values from -6 to 6
Outputs:
- features: bfloat16 [8, 256, 24, 576], P('sx', ('sy', 'af'))
- volume_grad: bfloat16 [8, 48, 48, 48, 128], P('af', 'sx', 'sy')
- kernel_grad: float32 [3, 3, 3, 128, 256], P(None, None, None, 'sx', ('sy', 'af'))
All inputs are finite; a program needn't handle non-finite values.
Results may differ from a plain program's by a relative error of at most 0.0025.
Values may be sent and summed in bfloat16 or wider, within the bound.
A program may use at most 64 MiB of HBM per device.

v0:
```python
import jax
import jax.numpy as jnp
from jax import lax
from jax.sharding import PartitionSpec as P


def from_behind(value, axis, steps):
    count = lax.axis_size(axis)
    leading, last = (max(0, -steps), min(count, count - steps))
    return lax.ppermute(value, axis, [(source, source + steps) for source in range(leading, last)])


def strided_patch(extended, tap_d, tap_h, tap_w, depth, height, width):
    return extended[
        :,
        tap_d : tap_d + 2 * depth : 2,
        tap_h : tap_h + 2 * height : 2,
        tap_w : tap_w + 2 * width : 2,
        :,
    ]


def parity_view(extended):
    samples, d_ext, h_ext, w_ext, channels = extended.shape
    pads = [(0, 0)] + [(0, n % 2) for n in (d_ext, h_ext, w_ext)] + [(0, 0)]
    even = jnp.pad(extended, pads)
    _, d2, h2, w2, _ = even.shape
    split = even.reshape(samples, d2 // 2, 2, h2 // 2, 2, w2 // 2, 2, channels)
    return split.transpose(2, 4, 6, 0, 1, 3, 5, 7)


def im2col(classes, depth, height, width):
    patches = []
    for tap_d in range(3):
        for tap_h in range(3):
            for tap_w in range(3):
                cls = classes[tap_d % 2, tap_h % 2, tap_w % 2]
                od, oh, ow = (tap_d // 2, tap_h // 2, tap_w // 2)
                patches.append(cls[:, od : od + depth, oh : oh + height, ow : ow + width, :])
    return jnp.concatenate(patches, axis=-1)


def weave(even_part, odd_part, axis):
    stacked = jnp.stack([even_part, odd_part], axis=axis + 1)
    shape = list(even_part.shape)
    shape[axis] = shape[axis] * 2
    return stacked.reshape(shape)


def spread_back(grad_space, kernel_full):
    samples, depth, height, width, filters = grad_space.shape
    channels = kernel_full.shape[3]
    grad_flat = grad_space.reshape(-1, filters)
    classes = {}
    for tap_d in range(3):
        for tap_h in range(3):
            for tap_w in range(3):
                term = lax.dot_general(
                    grad_flat,
                    kernel_full[tap_d, tap_h, tap_w],
                    (((1,), (1,)), ((), ())),
                    preferred_element_type=jnp.float32,
                )
                term = term.reshape(samples, depth, height, width, channels)
                pads = [(0, 0)]
                for tap in (tap_d, tap_h, tap_w):
                    pads.append((1, 0) if tap == 2 else (0, 1))
                pads.append((0, 0))
                term = jnp.pad(term, pads)
                key_name = (tap_d % 2, tap_h % 2, tap_w % 2)
                classes[key_name] = classes[key_name] + term if key_name in classes else term
    planes = []
    for parity_d in range(2):
        rows_h = []
        for parity_h in range(2):
            rows_h.append(weave(classes[parity_d, parity_h, 0], classes[parity_d, parity_h, 1], 3))
        planes.append(weave(rows_h[0], rows_h[1], 2))
    whole = weave(planes[0], planes[1], 1)
    return whole[:, : 2 * depth + 1, : 2 * height + 1, : 2 * width + 1, :]


def on_device(volume, kernel, cotangent):
    samples = volume.shape[0]
    depth = volume.shape[1] // 2
    height = volume.shape[2] // 2
    width = volume.shape[3] // 2
    n_sy = lax.axis_size("sy")
    n_af = lax.axis_size("af")
    kernel_part = lax.all_gather(kernel, ("sy", "af"), axis=4, tiled=True)
    kernel_full = lax.all_gather(kernel_part, "sx", axis=3, tiled=True)
    filters = kernel_full.shape[4]
    per_dev = filters // (n_sy * n_af)
    below = from_behind(volume[:, -1:], "sx", 1)
    extended = jnp.concatenate([below, volume], axis=1)
    beside = from_behind(extended[:, :, -1:], "sy", 1)
    extended = jnp.concatenate([beside, extended], axis=2)
    extended = jnp.pad(extended, ((0, 0), (0, 0), (0, 0), (1, 0), (0, 0)))
    rows = samples * depth * height * width
    classes = parity_view(extended)
    cols = im2col(classes, depth, height, width).reshape(rows, -1)
    kernel_mat = kernel_full.reshape(-1, filters)
    total = jnp.dot(cols, kernel_mat, preferred_element_type=jnp.float32)
    conv_space = total.astype(jnp.bfloat16).reshape(
        samples, depth, height, width, n_sy, n_af, per_dev
    )
    by_sample = lax.all_to_all(conv_space, "af", split_axis=5, concat_axis=0, tiled=True)
    gathered = lax.all_to_all(
        lax.all_to_all(by_sample, "sx", split_axis=0, concat_axis=1, tiled=True),
        "sy",
        split_axis=4,
        concat_axis=2,
        tiled=True,
    )
    own_samples = gathered.shape[0]
    edge_d = gathered.shape[1]
    edge_h = gathered.shape[2]
    features = (
        gathered.reshape(own_samples, edge_d, edge_h, width, per_dev)
        .transpose(0, 4, 1, 2, 3)
        .reshape(own_samples, per_dev, edge_d, edge_h * width)
    )
    grad_after = (
        cotangent.reshape(own_samples, per_dev, edge_d, edge_h, width)
        .transpose(0, 2, 3, 4, 1)
        .reshape(own_samples, edge_d, edge_h, width, 1, 1, per_dev)
    )
    grad_region = lax.all_to_all(
        lax.all_to_all(grad_after, "sx", split_axis=1, concat_axis=0, tiled=True),
        "sy",
        split_axis=2,
        concat_axis=4,
        tiled=True,
    )
    grad_back = lax.all_to_all(grad_region, "af", split_axis=0, concat_axis=5, tiled=True)
    grad_space = grad_back.reshape(samples, depth, height, width, filters)
    grad_flat = grad_space.reshape(rows, filters)
    kernel_terms = lax.dot_general(
        cols, grad_flat, (((0,), (0,)), ((), ())), preferred_element_type=jnp.float32
    )
    n_sx = lax.axis_size("sx")
    channels = kernel_full.shape[3]
    taps = kernel_terms.reshape(27, channels, n_sy * n_af, per_dev).transpose(2, 0, 1, 3)
    by_filter = lax.all_to_all(taps, ("sy", "af"), 0, 0, tiled=True).sum(axis=0)
    own_ch = channels // n_sx
    by_filter = by_filter.reshape(27, n_sx, own_ch, per_dev).transpose(1, 0, 2, 3)
    kernel_grad = lax.all_to_all(by_filter, "sx", 0, 0, tiled=True).sum(axis=0)
    kernel_grad = kernel_grad.reshape(3, 3, 3, own_ch, per_dev)
    partial_grad = spread_back(grad_space, kernel_full)
    from_above = from_behind(partial_grad[:, 0:1], "sx", -1)
    own_depth = partial_grad[:, 1:]
    own_depth = jnp.concatenate([own_depth[:, :-1], own_depth[:, -1:] + from_above], axis=1)
    from_right = from_behind(own_depth[:, :, 0:1].astype(jnp.bfloat16), "sy", -1).astype(
        jnp.float32
    )
    own_height = own_depth[:, :, 1:]
    own_height = jnp.concatenate(
        [own_height[:, :, :-1], own_height[:, :, -1:] + from_right], axis=2
    )
    volume_grad = own_height[:, :, :, 1:]
    return (features, volume_grad.astype(jnp.bfloat16), kernel_grad)


def solution(mesh):
    return jax.shard_map(
        on_device,
        mesh=mesh,
        in_specs=(
            P("af", "sx", "sy", None, None),
            P(None, None, None, "sx", ("sy", "af")),
            P("sx", ("sy", "af"), None, None),
        ),
        out_specs=(
            P("sx", ("sy", "af"), None, None),
            P("af", "sx", "sy", None, None),
            P(None, None, None, "sx", ("sy", "af")),
        ),
        check_vma=False,
    )
```

profile of v0, /device:TPU:96, one launch (start us, length us, event | category | flops | bytes accessed | tf_op | source)
XLA Modules:
  0.0 357.8 jit_solution(4887128388619679048)
XLA Ops:
  7.2 1.8 copy.579
  9.3 3.4 collective-permute-start
  12.8 6.2 %collective-permute-done = bf16[1,1,12,48,128]{4,1,3,2,0:T(2,128)(2,1)S(1)} collective-permute-done((bf16[1,1,12,48,128]{4,1,3,2,0:T(2,128)(2,1)S(1)}, bf16[1,1,12,48,128]{4,1,3,2,0:T(2,128)(2,1)S(1)}, u32[]{:S(2)}, u32[]{:S(2)}) %collective-permute-start) | collective-permute-done | bytes 147488 | tf_op jit(solution)/shard_map/ppermute | solution.py:10
  19.7 1.3 collective-permute-start.1
  21.0 40.2 %all_gather.6 = bf16[3,3,3,16,256]{3,4,2,1,0:T(8,128)(2,1)S(1)} all-gather(bf16[3,3,3,16,8]{3,4,2,1,0:T(8,128)(2,1)S(1)} %copy-done.8), channel_id=1, replica_groups=mesh['sx'=8,'sy'=4,'af'=8] {'sy','af'}, dimensions={4}, use_global_device_ids=true | all-gather | bytes 228096 | tf_op jit(solution)/shard_map/all_gather | solution.py:89
  61.3 1.3 copy.582
  62.6 2.0 reshape.220
  65.5 2.2 reshape.261
  67.7 18.5 %all-to-all-start.3 = ((bf16[8,2,6912]{2,1,0:T(2,128)(2,1)}), bf16[8,2,6912]{2,1,0:T(2,128)(2,1)S(1)}, u32[]{:S(2)}, u32[]{:S(2)}) async-start(bf16[8,2,6912]{2,1,0:T(2,128)(2,1)} %reshape.261), calls=%async_computation.3 | async-start | bytes 442368 | tf_op jit(solution)/shard_map/all_to_all | solution.py:128
  86.2 1.5 fusion.9
  88.0 2.1 fusion.16
  108.5 1.7 reshape.262
  110.5 2.2 reshape.263
  112.7 12.0 %all-to-all-start.4 = ((bf16[4,2,13824]{2,1,0:T(2,128)(2,1)}), bf16[4,2,13824]{2,1,0:T(2,128)(2,1)S(1)}, u32[]{:S(2)}, u32[]{:S(2)}) async-start(bf16[4,2,13824]{2,1,0:T(2,128)(2,1)} %reshape.263), calls=%async_computation.4 | async-start | bytes 442368 | tf_op jit(solution)/shard_map/all_to_all | solution.py:127
  124.7 0.8 slice_dynamic-update-slice_fusion.2
  125.5 0.8 slice_dynamic-update-slice_fusion.1
  126.2 10.7 %all-to-all-done.4 = bf16[4,2,13824]{2,1,0:T(2,128)(2,1)S(1)} async-done(((bf16[4,2,13824]{2,1,0:T(2,128)(2,1)}), bf16[4,2,13824]{2,1,0:T(2,128)(2,1)S(1)}, u32[]{:S(2)}, u32[]{:S(2)}) %all-to-all-start.4) | async-done | bytes 221216 | tf_op jit(solution)/shard_map/all_to_all | solution.py:127
  136.9 1.7 reshape.264
  138.9 2.2 reshape.265
  141.2 8.3 %all-to-all-start.5 = ((bf16[8,2,6912]{2,1,0:T(2,128)(2,1)}), bf16[8,2,6912]{2,1,0:T(2,128)(2,1)}, u32[]{:S(2)}, u32[]{:S(2)}) async-start(bf16[8,2,6912]{2,1,0:T(2,128)(2,1)} %reshape.265), calls=%async_computation.5 | async-start | bytes 442368 | tf_op jit(solution)/shard_map/all_to_all | solution.py:134
  150.2 4.0 %copy.581 = bf16[1,3,6,24,3456]{4,3,2,1,0:T(8,128)(2,1)} copy(bf16[1,3,6,24,3456]{4,1,3,2,0:T(4,128)(2,1)} %slice_dynamic-update-slice_fusion) | data formatting | bytes 5971968 | tf_op jit(solution)/shard_map/concatenate | solution.py:40
  154.2 4.3 %dot_general.205 = bf16[27,128,432]{1,0,2:T(8,128)(2,1)S(1)} reshape(bf16[3456,432]{0,1:T(8,128)(2,1)} %bitcast.438) | data formatting | bytes 5971968 | tf_op jit(solution)/shard_map/dot_general | solution.py:137
  158.5 3.6 %reshape.266 = bf16[8,1,3,4,6,8,24]{6,5,4,3,2,1,0:T(8,128)(2,1)} reshape(bf16[8,2,6912]{2,1,0:T(2,128)(2,1)} %all-to-all-done.5) | data formatting | bytes 442368
  162.2 4.0 %convolution_convert_fusion = bf16[432,256]{1,0:T(8,128)(2,1)} fusion(bf16[432,3456]{1,0:T(8,128)(2,1)} %bitcast.439, bf16[3456,256]{1,0:T(8,128)(2,1)} %bitcast.458), kind=kOutput, calls=%fused_computation.16 | convolution fusion | flops 764522496 | bytes 4976640 | tf_op jit(solution)/shard_map/dot_general | solution.py:102
  166.2 1.8 copy.583
  168.0 2.8 reshape.217
  170.8 2.7 copy.724
  173.5 3.5 reshape.255
  177.0 4.8 %all-to-all-start = ((bf16[8,2,6912]{2,1,0:T(2,128)(2,1)}), bf16[8,2,6912]{2,1,0:T(2,128)(2,1)}, u32[]{:S(2)}, u32[]{:S(2)}) async-start(bf16[8,2,6912]{2,1,0:T(2,128)(2,1)} %reshape.255), calls=%async_computation | async-start | bytes 442368 | tf_op jit(solution)/shard_map/all_to_all | solution.py:106
  181.8 1.3 bitcast_bitcast_fusion
  183.2 1.0 copy-done.1
  184.2 1.6 copy.628
  185.8 2.8 reshape_reshape.4
  189.0 3.6 %reshape.256 = bf16[8,1,3,6,4,8,24]{6,5,4,3,2,1,0:T(8,128)(2,1)} reshape(bf16[8,2,6912]{2,1,0:T(2,128)(2,1)} %all-to-all-done) | data formatting | bytes 442368
  192.7 2.5 fusion.17
  195.2 3.5 reshape.257
  198.7 9.4 %all-to-all-start.1 = ((bf16[8,2,6912]{2,1,0:T(2,128)(2,1)}), bf16[8,2,6912]{2,1,0:T(2,128)(2,1)}, u32[]{:S(2)}, u32[]{:S(2)}) async-start(bf16[8,2,6912]{2,1,0:T(2,128)(2,1)} %reshape.257), calls=%async_computation.1 | async-start | bytes 442368 | tf_op jit(solution)/shard_map/all_to_all | solution.py:108
  208.1 2.3 fusion.6
  210.4 3.9 %copy.631 = f32[32,27,128,8]{2,3,1,0:T(8,128)} copy(f32[32,27,128,8]{2,0,3,1:T(8,128)S(1)} %fusion.6) | data formatting | bytes 7077888 | tf_op jit(solution)/shard_map/transpose | solution.py:142
  214.2 4.9 %all-to-all-done.1 = bf16[8,2,6912]{2,1,0:T(2,128)(2,1)} async-done(((bf16[8,2,6912]{2,1,0:T(2,128)(2,1)}), bf16[8,2,6912]{2,1,0:T(2,128)(2,1)}, u32[]{:S(2)}, u32[]{:S(2)}) %all-to-all-start.1) | async-done | bytes 221216 | tf_op jit(solution)/shard_map/all_to_all | solution.py:108
  219.1 8.7 %all-to-all-start.6 = ((f32[32,27,128,8]{2,3,1,0:T(8,128)}), f32[32,27,128,8]{2,3,1,0:T(8,128)}, u32[]{:S(2)}, u32[]{:S(2)}) async-start(f32[32,27,128,8]{2,3,1,0:T(8,128)} %copy.631), calls=%async_computation.6 | async-start | bytes 7077888 | tf_op jit(solution)/shard_map/all_to_all | solution.py:143
  228.2 1.1 copy-done.5
  246.3 1.7 copy.627
  248.1 1.3 collective-permute-start.2
  249.8 3.6 %reshape.258 = bf16[8,3,6,4,1,8,24]{6,5,4,3,2,1,0:T(8,128)(2,1)} reshape(bf16[8,2,6912]{2,1,0:T(2,128)(2,1)} %all-to-all-done.1) | data formatting | bytes 442368
  253.5 2.5 copy_bitcast_fusion.10
  256.0 3.5 reshape.259
  259.5 53.2 %all-to-all-done.6 = f32[32,27,128,8]{2,3,1,0:T(8,128)} async-done(((f32[32,27,128,8]{2,3,1,0:T(8,128)}), f32[32,27,128,8]{2,3,1,0:T(8,128)}, u32[]{:S(2)}, u32[]{:S(2)}) %all-to-all-start.6) | async-done | bytes 3538976 | tf_op jit(solution)/shard_map/all_to_all | solution.py:143
  312.7 5.9 %all-to-all-start.2 = ((bf16[4,2,13824]{2,1,0:T(2,128)(2,1)}), bf16[4,2,13824]{2,1,0:T(2,128)(2,1)}, u32[]{:S(2)}, u32[]{:S(2)}) async-start(bf16[4,2,13824]{2,1,0:T(2,128)(2,1)} %reshape.259), calls=%async_computation.2 | async-start | bytes 442368 | tf_op jit(solution)/shard_map/all_to_all | solution.py:107
  318.6 2.2 slice_add_fusion
  322.2 3.1 collective-permute-start.3
  325.3 1.2 slice.381
  326.5 2.8 reduce_sum.18
  329.3 1.2 reshape.224
  330.5 1.5 copy.633
  332.0 2.2 reshape.267
  334.1 3.6 %all-to-all-start.7 = ((f32[8,1,3456]{2,1,0:T(1,128)}), f32[8,1,3456]{2,1,0:T(1,128)S(1)}, u32[]{:S(2)}, u32[]{:S(2)}) async-start(f32[8,1,3456]{2,1,0:T(1,128)} %reshape.267), calls=%async_computation.7 | async-start | bytes 221184 | tf_op jit(solution)/shard_map/all_to_all | solution.py:146
  337.8 1.0 fusion.15
  339.3 1.0 copy.635
  340.3 2.9 reshape.260
  343.6 1.5 reshape.219
  345.0 3.0 all-to-all-done.7
  348.6 0.9 reduce
  349.9 0.8 copy.634
  (116 shorter events, 43.2 us)
Async XLA Ops:
  7.2 13.9 %copy-start.8 = (bf16[3,3,3,16,8]{3,4,2,1,0:T(8,128)(2,1)S(1)}, bf16[3,3,3,16,8]{3,4,2,1,0:T(8,128)(2,1)}, u32[]{:S(2)}) copy-start(bf16[3,3,3,16,8]{3,4,2,1,0:T(8,128)(2,1)} %param.4) | copy-start | bytes 20740
  7.2 155.0 %all-gather.2.cloned.1.call-start = ((), (), s32[]{:S(2)}) async-start(), calls=%async_computation.8 | async-start | bytes 1990656 | tf_op jit(solution)/shard_map/all_gather | solution.py:90
  9.3 9.7 %collective-permute-start = (bf16[1,1,12,48,128]{4,1,3,2,0:T(2,128)(2,1)S(1)}, bf16[1,1,12,48,128]{4,1,3,2,0:T(2,128)(2,1)S(1)}, u32[]{:S(2)}, u32[]{:S(2)}) collective-permute-start(bf16[1,1,12,48,128]{4,1,3,2,0:T(2,128)(2,1)S(1)} %slice.315), channel_id=1, source_target_pairs={{0,32},{32,64},{64,96},{96,128},{128,160},{160,192},{192,224},{1,3... | collective-permute-start | bytes 442376 | tf_op jit(solution)/shard_map/ppermute | solution.py:10
  19.0 0.7 copy-start.6
  19.7 66.5 %collective-permute-start.1 = (bf16[1,7,1,48,128]{4,1,3,2,0:T(8,128)(2,1)}, bf16[1,7,1,48,128]{4,1,3,2,0:T(8,128)(2,1)}, u32[]{:S(2)}, u32[]{:S(2)}) collective-permute-start(bf16[1,7,1,48,128]{4,1,3,2,0:T(8,128)(2,1)} %pad_maximum_fusion.9), channel_id=1, source_target_pairs={{0,8},{8,16},{16,24},{1,9},{9,17},{17,25},{2,10},{10,18},{18,26},{... | collective-permute-start | bytes 258056 | tf_op jit(solution)/shard_map/ppermute | solution.py:10
  65.5 20.7 %copy-start.7 = (bf16[1,1,12,48,128]{4,1,3,2,0:T(2,128)(2,1)S(1)}, bf16[1,1,12,48,128]{4,1,3,2,0:T(2,128)(2,1)}, u32[]{:S(2)}) copy-start(bf16[1,1,12,48,128]{4,1,3,2,0:T(2,128)(2,1)} %copy-done.6) | copy-start | bytes 442372
  67.7 40.8 %all-to-all-start.3 = ((bf16[8,2,6912]{2,1,0:T(2,128)(2,1)}), bf16[8,2,6912]{2,1,0:T(2,128)(2,1)S(1)}, u32[]{:S(2)}, u32[]{:S(2)}) async-start(bf16[8,2,6912]{2,1,0:T(2,128)(2,1)} %reshape.261), calls=%async_computation.3 | async-start | bytes 442368 | tf_op jit(solution)/shard_map/all_to_all | solution.py:128
  112.7 24.2 %all-to-all-start.4 = ((bf16[4,2,13824]{2,1,0:T(2,128)(2,1)}), bf16[4,2,13824]{2,1,0:T(2,128)(2,1)S(1)}, u32[]{:S(2)}, u32[]{:S(2)}) async-start(bf16[4,2,13824]{2,1,0:T(2,128)(2,1)} %reshape.263), calls=%async_computation.4 | async-start | bytes 442368 | tf_op jit(solution)/shard_map/all_to_all | solution.py:127
  141.2 17.4 %all-to-all-start.5 = ((bf16[8,2,6912]{2,1,0:T(2,128)(2,1)}), bf16[8,2,6912]{2,1,0:T(2,128)(2,1)}, u32[]{:S(2)}, u32[]{:S(2)}) async-start(bf16[8,2,6912]{2,1,0:T(2,128)(2,1)} %reshape.265), calls=%async_computation.5 | async-start | bytes 442368 | tf_op jit(solution)/shard_map/all_to_all | solution.py:134
  177.0 12.0 %all-to-all-start = ((bf16[8,2,6912]{2,1,0:T(2,128)(2,1)}), bf16[8,2,6912]{2,1,0:T(2,128)(2,1)}, u32[]{:S(2)}, u32[]{:S(2)}) async-start(bf16[8,2,6912]{2,1,0:T(2,128)(2,1)} %reshape.255), calls=%async_computation | async-start | bytes 442368 | tf_op jit(solution)/shard_map/all_to_all | solution.py:106
  183.2 1.0 copy-start.1
  198.7 20.4 %all-to-all-start.1 = ((bf16[8,2,6912]{2,1,0:T(2,128)(2,1)}), bf16[8,2,6912]{2,1,0:T(2,128)(2,1)}, u32[]{:S(2)}, u32[]{:S(2)}) async-start(bf16[8,2,6912]{2,1,0:T(2,128)(2,1)} %reshape.257), calls=%async_computation.1 | async-start | bytes 442368 | tf_op jit(solution)/shard_map/all_to_all | solution.py:108
  214.2 13.6 %copy-start.2 = (bf16[1,3,6,24,4,8,1,8]{3,7,2,4,1,5,6,0:T(8,128)(2,1)S(1)}, bf16[1,3,6,24,4,8,1,8]{3,7,2,4,1,5,6,0:T(8,128)(2,1)}, u32[]{:S(2)}) copy-start(bf16[1,3,6,24,4,8,1,8]{3,7,2,4,1,5,6,0:T(8,128)(2,1)} %copy-done.1) | copy-start | bytes 663556
  219.1 93.5 %all-to-all-start.6 = ((f32[32,27,128,8]{2,3,1,0:T(8,128)}), f32[32,27,128,8]{2,3,1,0:T(8,128)}, u32[]{:S(2)}, u32[]{:S(2)}) async-start(f32[32,27,128,8]{2,3,1,0:T(8,128)} %copy.631), calls=%async_computation.6 | async-start | bytes 7077888 | tf_op jit(solution)/shard_map/all_to_all | solution.py:143
  227.8 1.5 copy-start.5
  247.9 1.6 copy-start
  248.1 70.4 %collective-permute-start.2 = (f32[1,1,13,49,128]{4,1,3,2,0:T(1,128)S(1)}, f32[1,1,13,49,128]{4,1,3,2,0:T(1,128)S(1)}, u32[]{:S(2)}, u32[]{:S(2)}) collective-permute-start(f32[1,1,13,49,128]{4,1,3,2,0:T(1,128)S(1)} %slice.380), channel_id=1, source_target_pairs={{32,0},{64,32},{96,64},{128,96},{160,128},{192,160},{224,192},{33,... | collective-permute-start | bytes 978440 | tf_op jit(solution)/shard_map/ppermute | solution.py:10
  312.7 21.4 %all-to-all-start.2 = ((bf16[4,2,13824]{2,1,0:T(2,128)(2,1)}), bf16[4,2,13824]{2,1,0:T(2,128)(2,1)}, u32[]{:S(2)}, u32[]{:S(2)}) async-start(bf16[4,2,13824]{2,1,0:T(2,128)(2,1)} %reshape.259), calls=%async_computation.2 | async-start | bytes 442368 | tf_op jit(solution)/shard_map/all_to_all | solution.py:107
  320.8 0.7 copy-start.4
  322.2 15.6 %collective-permute-start.3 = (bf16[1,6,1,49,128]{4,1,3,2,0:T(8,128)(2,1)}, bf16[1,6,1,49,128]{4,1,3,2,0:T(8,128)(2,1)}, u32[]{:S(2)}, u32[]{:S(2)}) collective-permute-start(bf16[1,6,1,49,128]{4,1,3,2,0:T(8,128)(2,1)} %slice.384), channel_id=1, source_target_pairs={{8,0},{16,8},{24,16},{9,1},{17,9},{25,17},{10,2},{18,10},{26,18},{... | collective-permute-start | bytes 225800 | tf_op jit(solution)/shard_map/ppermute | solution.py:10
  334.1 13.9 %all-to-all-start.7 = ((f32[8,1,3456]{2,1,0:T(1,128)}), f32[8,1,3456]{2,1,0:T(1,128)S(1)}, u32[]{:S(2)}, u32[]{:S(2)}) async-start(f32[8,1,3456]{2,1,0:T(1,128)} %reshape.267), calls=%async_computation.7 | async-start | bytes 221184 | tf_op jit(solution)/shard_map/all_to_all | solution.py:146
  337.7 1.3 copy-start.3
Sparse Core Ops, SparseCore 0:
  62.8 88.7 all-gather.1
where the time goes:
time: 364 us; the launch traced here: 358 us
  local copies, waits for them, and re-layouts  113 us (31%)
  starting transfers between devices  80.2 us (22%)
  waiting for transfers between devices  78.5 us (22%)
  blocking collectives  40.2 us (11%)
  matrix products  18.7 us (5%)
  between operations  14.8 us (4%)
  other arithmetic  12.6 us (3%)
    unnamed x66, local copies, waits for them, and re-layouts  67.3 us
    all_to_all x1, waiting for transfers between devices, on_device(): by_filter = lax.all_to_all(taps, ('sy', 'af'), 0, 0, tiled=True).sum(axis=0)  53.2 us
    all_gather x1, blocking collectives, on_device(): kernel_part = lax.all_gather(kernel, ('sy', 'af'), axis=4, tiled=True)  40.2 us
    all_to_all x1, starting transfers between devices, on_device(): lax.all_to_all(grad_after, 'sx', split_axis=1, concat_axis=0, tiled=True)  18.5 us
    dot_general x27, matrix products, spread_back(): lax.dot_general(grad_flat, kernel_full[tap_d, tap_h, tap_w], (((1,), (1,)...  12.4 us
    all_to_all x1, starting transfers between devices, on_device(): lax.all_to_all(lax.all_to_all(grad_after, 'sx', split_axis=1, concat_axis...  12 us
    all_to_all x1, waiting for transfers between devices, on_device(): lax.all_to_all(lax.all_to_all(grad_after, 'sx', split_axis=1, concat_axis...  10.7 us
    all_to_all x1, starting transfers between devices, on_device(): lax.all_to_all(by_sample, 'sx', split_axis=0, concat_axis=1, tiled=True)  9.37 us
  transfers between devices with their start and end apart: 13, of which 6 were waited for; matrix products, arithmetic and copies ran while one was open for 31% of the time, Pallas kernels for 0%

commit v1 on v0

--- a/solution.py
+++ b/solution.py
@@ -87,7 +87,9 @@
     n_sy = lax.axis_size("sy")
     n_af = lax.axis_size("af")
     kernel_part = lax.all_gather(kernel, ("sy", "af"), axis=4, tiled=True)
-    kernel_full = lax.all_gather(kernel_part, "sx", axis=3, tiled=True)
+    kernel_full = jnp.concatenate(
+        lax.all_to_all(jnp.stack([kernel_part] * lax.axis_size("sx")), "sx", 0, 0), axis=3
+    )
     filters = kernel_full.shape[4]
     per_dev = filters // (n_sy * n_af)
     below = from_behind(volume[:, -1:], "sx", 1)

time: 364 us -> 367 us (level)
  waiting for transfers between devices: 78.5 us -> 93.5 us
  between operations: 14.8 us -> 1.48 us
  local copies, waits for them, and re-layouts: 113 us -> 120 us
  starting transfers between devices: 80.2 us -> 76.4 us
    all_to_all x0 -> x1, waiting for transfers between devices: none -> 20.5 us  [on_device(): lax.all_to_all(jnp.stack([kernel_part] * lax.axis_size('sx')), 'sx', 0, 0)]
    all_to_all x0 -> x1, starting transfers between devices: none -> 16 us  [on_device(): lax.all_to_all(jnp.stack([kernel_part] * lax.axis_size('sx')), 'sx', 0, 0)]
    all_to_all x1, starting transfers between devices: 18.5 us -> 7.24 us  [on_device(): lax.all_to_all(grad_after, 'sx', split_axis=1, concat_axis=0, tiled=True)]
    all_to_all x1, waiting for transfers between devices: 0.01 us -> 6.27 us  [on_device(): lax.all_to_all(grad_region, 'af', split_axis=0, concat_axis=5, tiled=True)]
    ppermute x4, waiting for transfers between devices: 6.24 us -> 0.01 us  [from_behind(): lax.ppermute(value, axis, [(source, source + steps) for source in range(l...]
    all_to_all x1, waiting for transfers between devices: 10.7 us -> 4.82 us  [on_device(): lax.all_to_all(lax.all_to_all(grad_after, 'sx', split_axis=1, concat_axis...]
    all_to_all x1, starting transfers between devices: 9.37 us -> 4.14 us  [on_device(): lax.all_to_all(by_sample, 'sx', split_axis=0, concat_axis=1, tiled=True)]
    all_to_all x1, starting transfers between devices: 8.28 us -> 3.4 us  [on_device(): lax.all_to_all(grad_region, 'af', split_axis=0, concat_axis=5, tiled=True)]
  transfers between devices with their start and end apart: 13 -> 13, of which waited for: 6 -> 7; matrix products, arithmetic and copies ran while one was open for 31% -> 29% of each run, Pallas kernels for 0% -> 0%
where the time goes in v1:
time: 367 us; the launch traced here: 361 us
  local copies, waits for them, and re-layouts  120 us (33%)
  waiting for transfers between devices  93.5 us (25%)
  starting transfers between devices  76.4 us (21%)
  blocking collectives  40.4 us (11%)
  matrix products  16.4 us (4%)
  other arithmetic  12.6 us (3%)
    unnamed x86, local copies, waits for them, and re-layouts  71.5 us
    all_to_all x1, waiting for transfers between devices, on_device(): by_filter = lax.all_to_all(taps, ('sy', 'af'), 0, 0, tiled=True).sum(axis=0)  53.3 us
    all_gather x1, blocking collectives, on_device(): kernel_part = lax.all_gather(kernel, ('sy', 'af'), axis=4, tiled=True)  40.4 us
    all_to_all x1, waiting for transfers between devices, on_device(): lax.all_to_all(jnp.stack([kernel_part] * lax.axis_size('sx')), 'sx', 0, 0)  20.5 us
    all_to_all x1, starting transfers between devices, on_device(): lax.all_to_all(jnp.stack([kernel_part] * lax.axis_size('sx')), 'sx', 0, 0)  16 us
    dot_general x27, matrix products, spread_back(): lax.dot_general(grad_flat, kernel_full[tap_d, tap_h, tap_w], (((1,), (1,)...  12.4 us
    all_to_all x1, starting transfers between devices, on_device(): lax.all_to_all(lax.all_to_all(grad_after, 'sx', split_axis=1, concat_axis...  12 us
    all_to_all x1, starting transfers between devices, on_device(): by_filter = lax.all_to_all(taps, ('sy', 'af'), 0, 0, tiled=True).sum(axis=0)  9.9 us
  transfers between devices with their start and end apart: 13, of which 7 were waited for; matrix products, arithmetic and copies ran while one was open for 29% of the time, Pallas kernels for 0%

profile of v1, /device:TPU:96, one launch (start us, length us, event | category | flops | bytes accessed | tf_op | source)
XLA Modules:
  0.0 361.1 jit_solution(9776258515263094517)
XLA Ops:
  0.6 1.8 copy.582
  2.5 1.0 slice.315
  3.5 4.1 %collective-permute-start = (bf16[1,1,12,48,128]{4,1,3,2,0:T(2,128)(2,1)}, bf16[1,1,12,48,128]{4,1,3,2,0:T(2,128)(2,1)}, u32[]{:S(2)}, u32[]{:S(2)}) collective-permute-start(bf16[1,1,12,48,128]{4,1,3,2,0:T(2,128)(2,1)} %slice.315), channel_id=1, source_target_pairs={{0,32},{32,64},{64,96},{96,128},{128,160},{160,192},{192,224},{1,3... | collective-permute-start | bytes 442376 | tf_op jit(solution)/shard_map/ppermute | solution.py:10
  9.4 2.3 reshape.267
  11.6 7.2 %all-to-all-start.4 = ((bf16[8,2,6912]{2,1,0:T(2,128)(2,1)}), bf16[8,2,6912]{2,1,0:T(2,128)(2,1)}, u32[]{:S(2)}, u32[]{:S(2)}) async-start(bf16[8,2,6912]{2,1,0:T(2,128)(2,1)} %reshape.267), calls=%async_computation.4 | async-start | bytes 442368 | tf_op jit(solution)/shard_map/all_to_all | solution.py:130
  19.7 1.3 collective-permute-start.1
  21.0 40.4 %all_gather.3 = bf16[3,3,3,16,256]{3,4,2,1,0:T(8,128)(2,1)S(1)} all-gather(bf16[3,3,3,16,8]{3,4,2,1,0:T(8,128)(2,1)S(1)} %copy-done.18), channel_id=1, replica_groups=mesh['sx'=8,'sy'=4,'af'=8] {'sy','af'}, dimensions={4}, use_global_device_ids=true | all-gather | bytes 228096 | tf_op jit(solution)/shard_map/all_gather | solution.py:89
  61.4 1.3 copy.585
  62.8 1.6 fusion.9
  64.6 2.7 fusion.16
  76.0 2.9 reshape.268
  79.2 2.3 reshape.269
  81.5 12.0 %all-to-all-start.5 = ((bf16[4,2,13824]{2,1,0:T(2,128)(2,1)}), bf16[4,2,13824]{2,1,0:T(2,128)(2,1)S(1)}, u32[]{:S(2)}, u32[]{:S(2)}) async-start(bf16[4,2,13824]{2,1,0:T(2,128)(2,1)} %reshape.269), calls=%async_computation.5 | async-start | bytes 442368 | tf_op jit(solution)/shard_map/all_to_all | solution.py:129
  95.1 4.8 %all-to-all-done.5 = bf16[4,2,13824]{2,1,0:T(2,128)(2,1)S(1)} async-done(((bf16[4,2,13824]{2,1,0:T(2,128)(2,1)}), bf16[4,2,13824]{2,1,0:T(2,128)(2,1)S(1)}, u32[]{:S(2)}, u32[]{:S(2)}) %all-to-all-start.5) | async-done | bytes 221216 | tf_op jit(solution)/shard_map/all_to_all | solution.py:129
  99.9 1.7 reshape.270
  101.9 2.2 reshape.271
  104.2 3.4 all-to-all-start.6
  108.3 6.3 %all-to-all-done.6 = bf16[8,2,6912]{2,1,0:T(2,128)(2,1)S(1)} async-done(((bf16[8,2,6912]{2,1,0:T(2,128)(2,1)}), bf16[8,2,6912]{2,1,0:T(2,128)(2,1)S(1)}, u32[]{:S(2)}, u32[]{:S(2)}) %all-to-all-start.6) | async-done | bytes 221216 | tf_op jit(solution)/shard_map/all_to_all | solution.py:136
  115.3 1.3 stack.56
  116.6 16.0 %all-to-all-start = ((bf16[8,3,3,3,16,256]{5,4,3,2,1,0:T(8,128)(2,1)}), bf16[8,3,3,3,16,256]{5,4,3,2,1,0:T(8,128)(2,1)}, u32[]{:S(2)}, u32[]{:S(2)}) async-start(bf16[8,3,3,3,16,256]{5,4,3,2,1,0:T(8,128)(2,1)} %stack.56), calls=%async_computation | async-start | bytes 3538944 | tf_op jit(solution)/shard_map/all_to_all | solution.py:91
  143.2 4.1 %copy.584 = bf16[1,3,6,24,3456]{4,3,2,1,0:T(8,128)(2,1)} copy(bf16[1,3,6,24,3456]{4,1,3,2,0:T(4,128)(2,1)} %slice_dynamic-update-slice_fusion) | data formatting | bytes 5971968 | tf_op jit(solution)/shard_map/concatenate | solution.py:40
  147.3 4.3 %dot_general.205 = bf16[27,128,432]{1,0,2:T(8,128)(2,1)S(1)} reshape(bf16[3456,432]{0,1:T(8,128)(2,1)} %bitcast.442) | data formatting | bytes 5971968 | tf_op jit(solution)/shard_map/dot_general | solution.py:139
  151.6 3.6 %reshape.272 = bf16[8,1,3,4,6,8,24]{6,5,4,3,2,1,0:T(8,128)(2,1)} reshape(bf16[8,2,6912]{2,1,0:T(2,128)(2,1)} %copy-done.14) | data formatting | bytes 442368
  155.2 20.5 %all-to-all-done = bf16[8,3,3,3,16,256]{5,4,3,2,1,0:T(8,128)(2,1)} async-done(((bf16[8,3,3,3,16,256]{5,4,3,2,1,0:T(8,128)(2,1)}), bf16[8,3,3,3,16,256]{5,4,3,2,1,0:T(8,128)(2,1)}, u32[]{:S(2)}, u32[]{:S(2)}) %all-to-all-start) | async-done | bytes 1769504 | tf_op jit(solution)/shard_map/all_to_all | solution.py:91
  175.7 1.8 copy.586
  177.5 1.3 copy-done.4
  178.8 1.7 convolution_convert_fusion
  180.5 1.8 copy.587
  182.2 2.8 reshape.222
  185.1 2.7 copy.728
  187.7 3.5 reshape.261
  191.3 4.4 %all-to-all-start.1 = ((bf16[8,2,6912]{2,1,0:T(2,128)(2,1)}), bf16[8,2,6912]{2,1,0:T(2,128)(2,1)}, u32[]{:S(2)}, u32[]{:S(2)}) async-start(bf16[8,2,6912]{2,1,0:T(2,128)(2,1)} %reshape.261), calls=%async_computation.1 | async-start | bytes 442368 | tf_op jit(solution)/shard_map/all_to_all | solution.py:108
  195.7 1.3 bitcast_bitcast_fusion
  198.0 1.6 copy.632
  199.6 2.8 reshape_reshape.8
  202.8 3.6 %reshape.262 = bf16[8,1,3,6,4,8,24]{6,5,4,3,2,1,0:T(8,128)(2,1)} reshape(bf16[8,2,6912]{2,1,0:T(2,128)(2,1)} %all-to-all-done.1) | data formatting | bytes 442368
  206.4 2.5 fusion.17
  208.9 3.5 reshape.263
  212.4 4.1 %all-to-all-start.2 = ((bf16[8,2,6912]{2,1,0:T(2,128)(2,1)}), bf16[8,2,6912]{2,1,0:T(2,128)(2,1)}, u32[]{:S(2)}, u32[]{:S(2)}) async-start(bf16[8,2,6912]{2,1,0:T(2,128)(2,1)} %reshape.263), calls=%async_computation.2 | async-start | bytes 442368 | tf_op jit(solution)/shard_map/all_to_all | solution.py:110
  216.6 2.3 fusion.6
  218.9 3.8 %copy.635 = f32[32,27,128,8]{2,3,1,0:T(8,128)} copy(f32[32,27,128,8]{2,0,3,1:T(8,128)S(1)} %fusion.6) | data formatting | bytes 7077888 | tf_op jit(solution)/shard_map/transpose | solution.py:144
  222.8 5.3 %all-to-all-done.2 = bf16[8,2,6912]{2,1,0:T(2,128)(2,1)} async-done(((bf16[8,2,6912]{2,1,0:T(2,128)(2,1)}), bf16[8,2,6912]{2,1,0:T(2,128)(2,1)}, u32[]{:S(2)}, u32[]{:S(2)}) %all-to-all-start.2) | async-done | bytes 221216 | tf_op jit(solution)/shard_map/all_to_all | solution.py:110
  228.0 9.9 %all-to-all-start.7 = ((f32[32,27,128,8]{2,3,1,0:T(8,128)}), f32[32,27,128,8]{2,3,1,0:T(8,128)}, u32[]{:S(2)}, u32[]{:S(2)}) async-start(f32[32,27,128,8]{2,3,1,0:T(8,128)} %copy.635), calls=%async_computation.7 | async-start | bytes 7077888 | tf_op jit(solution)/shard_map/all_to_all | solution.py:145
  238.3 1.1 copy-done.5
  256.3 1.7 copy.631
  258.2 1.3 collective-permute-start.2
  259.8 3.6 %reshape.264 = bf16[8,3,6,4,1,8,24]{6,5,4,3,2,1,0:T(8,128)(2,1)} reshape(bf16[8,2,6912]{2,1,0:T(2,128)(2,1)} %all-to-all-done.2) | data formatting | bytes 442368
  263.5 2.5 copy_bitcast_fusion.10
  266.0 3.5 reshape.265
  269.5 53.3 %all-to-all-done.7 = f32[32,27,128,8]{2,3,1,0:T(8,128)} async-done(((f32[32,27,128,8]{2,3,1,0:T(8,128)}), f32[32,27,128,8]{2,3,1,0:T(8,128)}, u32[]{:S(2)}, u32[]{:S(2)}) %all-to-all-start.7) | async-done | bytes 3538976 | tf_op jit(solution)/shard_map/all_to_all | solution.py:145
  322.8 5.9 %all-to-all-start.3 = ((bf16[4,2,13824]{2,1,0:T(2,128)(2,1)}), bf16[4,2,13824]{2,1,0:T(2,128)(2,1)}, u32[]{:S(2)}, u32[]{:S(2)}) async-start(bf16[4,2,13824]{2,1,0:T(2,128)(2,1)} %reshape.265), calls=%async_computation.3 | async-start | bytes 442368 | tf_op jit(solution)/shard_map/all_to_all | solution.py:109
  328.7 2.2 slice_add_fusion
  332.3 3.1 collective-permute-start.3
  335.4 1.2 slice.381
  336.6 2.8 reduce_sum.18
  339.4 1.2 reshape.230
  340.6 1.5 copy.637
  342.1 2.2 reshape.273
  344.2 3.6 %all-to-all-start.8 = ((f32[8,1,3456]{2,1,0:T(1,128)}), f32[8,1,3456]{2,1,0:T(1,128)S(1)}, u32[]{:S(2)}, u32[]{:S(2)}) async-start(f32[8,1,3456]{2,1,0:T(1,128)} %reshape.273), calls=%async_computation.8 | async-start | bytes 221184 | tf_op jit(solution)/shard_map/all_to_all | solution.py:148
  347.9 1.0 fusion.15
  349.4 1.0 copy.639
  350.4 2.9 reshape.266
  353.7 1.5 reshape.224
  355.1 3.0 all-to-all-done.8
  (137 shorter events, 49.3 us)
Async XLA Ops:
  0.6 7.0 %copy-start.17 = (bf16[1,8,24,576]{3,2,1,0:T(8,128)(2,1)S(1)}, bf16[1,8,24,576]{3,2,1,0:T(8,128)(2,1)}, u32[]{:S(2)}) copy-start(bf16[1,8,24,576]{3,2,1,0:T(8,128)(2,1)} %param.5) | copy-start | bytes 663556
  3.5 15.4 %collective-permute-start = (bf16[1,1,12,48,128]{4,1,3,2,0:T(2,128)(2,1)}, bf16[1,1,12,48,128]{4,1,3,2,0:T(2,128)(2,1)}, u32[]{:S(2)}, u32[]{:S(2)}) collective-permute-start(bf16[1,1,12,48,128]{4,1,3,2,0:T(2,128)(2,1)} %slice.315), channel_id=1, source_target_pairs={{0,32},{32,64},{64,96},{96,128},{128,160},{160,192},{192,224},{1,3... | collective-permute-start | bytes 442376 | tf_op jit(solution)/shard_map/ppermute | solution.py:10
  9.4 11.6 %copy-start.18 = (bf16[3,3,3,16,8]{3,4,2,1,0:T(8,128)(2,1)S(1)}, bf16[3,3,3,16,8]{3,4,2,1,0:T(8,128)(2,1)}, u32[]{:S(2)}) copy-start(bf16[3,3,3,16,8]{3,4,2,1,0:T(8,128)(2,1)} %param.4) | copy-start | bytes 20740
  11.6 64.3 %all-to-all-start.4 = ((bf16[8,2,6912]{2,1,0:T(2,128)(2,1)}), bf16[8,2,6912]{2,1,0:T(2,128)(2,1)}, u32[]{:S(2)}, u32[]{:S(2)}) async-start(bf16[8,2,6912]{2,1,0:T(2,128)(2,1)} %reshape.267), calls=%async_computation.4 | async-start | bytes 442368 | tf_op jit(solution)/shard_map/all_to_all | solution.py:130
  19.7 43.1 %collective-permute-start.1 = (bf16[1,7,1,48,128]{4,1,3,2,0:T(8,128)(2,1)S(1)}, bf16[1,7,1,48,128]{4,1,3,2,0:T(8,128)(2,1)S(1)}, u32[]{:S(2)}, u32[]{:S(2)}) collective-permute-start(bf16[1,7,1,48,128]{4,1,3,2,0:T(8,128)(2,1)S(1)} %pad_maximum_fusion.9), channel_id=1, source_target_pairs={{0,8},{8,16},{16,24},{1,9},{9,17},{17,25},{2,10},{10,18},{18,26},{... | collective-permute-start | bytes 258056 | tf_op jit(solution)/shard_map/ppermute | solution.py:10
  69.8 4.5 %copy-start.9 = (bf16[1,4,7,25,128]{4,1,3,2,0:T(4,128)(2,1)}, bf16[1,4,7,25,128]{4,1,3,2,0:T(4,128)(2,1)S(1)}, u32[]{:S(2)}) copy-start(bf16[1,4,7,25,128]{4,1,3,2,0:T(4,128)(2,1)S(1)} %get-tuple-element.45) | copy-start | bytes 537604
  74.4 1.5 copy-start.11
  79.2 15.0 %copy-start.8 = (bf16[1,1,1,1,4,7,25,128]{7,0,4,2,6,1,5,3:T(2,128)(2,1)S(1)}, bf16[1,1,1,1,4,7,25,128]{7,0,4,2,6,1,5,3:T(2,128)(2,1)}, u32[]{:S(2)}) copy-start(bf16[1,1,1,1,4,7,25,128]{7,0,4,2,6,1,5,3:T(2,128)(2,1)} %get-tuple-element.34) | copy-start | bytes 537604
  81.5 18.5 %all-to-all-start.5 = ((bf16[4,2,13824]{2,1,0:T(2,128)(2,1)}), bf16[4,2,13824]{2,1,0:T(2,128)(2,1)S(1)}, u32[]{:S(2)}, u32[]{:S(2)}) async-start(bf16[4,2,13824]{2,1,0:T(2,128)(2,1)} %reshape.269), calls=%async_computation.5 | async-start | bytes 442368 | tf_op jit(solution)/shard_map/all_to_all | solution.py:129
  101.6 6.0 %copy-start.13 = (bf16[1,4,7,25,128]{4,1,3,2,0:T(4,128)(2,1)S(1)}, bf16[1,4,7,25,128]{4,1,3,2,0:T(4,128)(2,1)}, u32[]{:S(2)}) copy-start(bf16[1,4,7,25,128]{4,1,3,2,0:T(4,128)(2,1)} %get-tuple-element.42) | copy-start | bytes 537604
  101.6 13.7 %copy-start.15 = (bf16[3,3,3,16,256]{4,3,2,1,0:T(8,128)(2,1)S(1)}, bf16[3,3,3,16,256]{4,3,2,1,0:T(8,128)(2,1)}, u32[]{:S(2)}) copy-start(bf16[3,3,3,16,256]{4,3,2,1,0:T(8,128)(2,1)} %copy.585) | copy-start | bytes 663556
  104.2 10.4 %all-to-all-start.6 = ((bf16[8,2,6912]{2,1,0:T(2,128)(2,1)}), bf16[8,2,6912]{2,1,0:T(2,128)(2,1)S(1)}, u32[]{:S(2)}, u32[]{:S(2)}) async-start(bf16[8,2,6912]{2,1,0:T(2,128)(2,1)} %reshape.271), calls=%async_computation.6 | async-start | bytes 442368 | tf_op jit(solution)/shard_map/all_to_all | solution.py:136
  114.6 0.7 copy-start.14
  116.6 16.0 %copy-start.16 = (bf16[1,4,7,25,128]{4,1,3,2,0:T(4,128)(2,1)S(1)}, bf16[1,4,7,25,128]{4,1,3,2,0:T(4,128)(2,1)}, u32[]{:S(2)}) copy-start(bf16[1,4,7,25,128]{4,1,3,2,0:T(4,128)(2,1)} %get-tuple-element.41) | copy-start | bytes 537604
  116.6 18.2 %copy-start.12 = (bf16[1,4,7,25,128]{4,1,3,2,0:T(4,128)(2,1)S(1)}, bf16[1,4,7,25,128]{4,1,3,2,0:T(4,128)(2,1)}, u32[]{:S(2)}) copy-start(bf16[1,4,7,25,128]{4,1,3,2,0:T(4,128)(2,1)} %copy-done.11) | copy-start | bytes 537604
  116.6 59.1 %all-to-all-start = ((bf16[8,3,3,3,16,256]{5,4,3,2,1,0:T(8,128)(2,1)}), bf16[8,3,3,3,16,256]{5,4,3,2,1,0:T(8,128)(2,1)}, u32[]{:S(2)}, u32[]{:S(2)}) async-start(bf16[8,3,3,3,16,256]{5,4,3,2,1,0:T(8,128)(2,1)} %stack.56), calls=%async_computation | async-start | bytes 3538944 | tf_op jit(solution)/shard_map/all_to_all | solution.py:91
  132.6 6.8 %copy-start.10 = (bf16[1,4,7,25,128]{4,1,3,2,0:T(4,128)(2,1)S(1)}, bf16[1,4,7,25,128]{4,1,3,2,0:T(4,128)(2,1)}, u32[]{:S(2)}) copy-start(bf16[1,4,7,25,128]{4,1,3,2,0:T(4,128)(2,1)} %copy-done.9) | copy-start | bytes 537604
  175.7 3.1 copy-start.1
  177.5 1.3 copy-start.4
  191.3 11.5 %all-to-all-start.1 = ((bf16[8,2,6912]{2,1,0:T(2,128)(2,1)}), bf16[8,2,6912]{2,1,0:T(2,128)(2,1)}, u32[]{:S(2)}, u32[]{:S(2)}) async-start(bf16[8,2,6912]{2,1,0:T(2,128)(2,1)} %reshape.261), calls=%async_computation.1 | async-start | bytes 442368 | tf_op jit(solution)/shard_map/all_to_all | solution.py:108
  197.0 1.0 copy-start.2
  212.4 15.6 %all-to-all-start.2 = ((bf16[8,2,6912]{2,1,0:T(2,128)(2,1)}), bf16[8,2,6912]{2,1,0:T(2,128)(2,1)}, u32[]{:S(2)}, u32[]{:S(2)}) async-start(bf16[8,2,6912]{2,1,0:T(2,128)(2,1)} %reshape.263), calls=%async_computation.2 | async-start | bytes 442368 | tf_op jit(solution)/shard_map/all_to_all | solution.py:110
  222.8 15.2 %copy-start.3 = (bf16[1,3,6,24,4,8,1,8]{3,7,2,4,1,5,6,0:T(8,128)(2,1)S(1)}, bf16[1,3,6,24,4,8,1,8]{3,7,2,4,1,5,6,0:T(8,128)(2,1)}, u32[]{:S(2)}) copy-start(bf16[1,3,6,24,4,8,1,8]{3,7,2,4,1,5,6,0:T(8,128)(2,1)} %copy-done.2) | copy-start | bytes 663556
  228.0 94.8 %all-to-all-start.7 = ((f32[32,27,128,8]{2,3,1,0:T(8,128)}), f32[32,27,128,8]{2,3,1,0:T(8,128)}, u32[]{:S(2)}, u32[]{:S(2)}) async-start(f32[32,27,128,8]{2,3,1,0:T(8,128)} %copy.635), calls=%async_computation.7 | async-start | bytes 7077888 | tf_op jit(solution)/shard_map/all_to_all | solution.py:145
  238.0 1.5 copy-start.5
  258.0 1.6 copy-start
  258.2 70.6 %collective-permute-start.2 = (f32[1,1,13,49,128]{4,1,3,2,0:T(1,128)S(1)}, f32[1,1,13,49,128]{4,1,3,2,0:T(1,128)S(1)}, u32[]{:S(2)}, u32[]{:S(2)}) collective-permute-start(f32[1,1,13,49,128]{4,1,3,2,0:T(1,128)S(1)} %slice.380), channel_id=1, source_target_pairs={{32,0},{64,32},{96,64},{128,96},{160,128},{192,160},{224,192},{33,... | collective-permute-start | bytes 978440 | tf_op jit(solution)/shard_map/ppermute | solution.py:10
  322.8 21.4 %all-to-all-start.3 = ((bf16[4,2,13824]{2,1,0:T(2,128)(2,1)}), bf16[4,2,13824]{2,1,0:T(2,128)(2,1)}, u32[]{:S(2)}, u32[]{:S(2)}) async-start(bf16[4,2,13824]{2,1,0:T(2,128)(2,1)} %reshape.265), calls=%async_computation.3 | async-start | bytes 442368 | tf_op jit(solution)/shard_map/all_to_all | solution.py:109
  330.9 0.7 copy-start.7
  332.3 15.6 %collective-permute-start.3 = (bf16[1,6,1,49,128]{4,1,3,2,0:T(8,128)(2,1)}, bf16[1,6,1,49,128]{4,1,3,2,0:T(8,128)(2,1)}, u32[]{:S(2)}, u32[]{:S(2)}) collective-permute-start(bf16[1,6,1,49,128]{4,1,3,2,0:T(8,128)(2,1)} %slice.384), channel_id=1, source_target_pairs={{8,0},{16,8},{24,16},{9,1},{17,9},{25,17},{10,2},{18,10},{26,18},{... | collective-permute-start | bytes 225800 | tf_op jit(solution)/shard_map/ppermute | solution.py:10
  344.2 13.9 %all-to-all-start.8 = ((f32[8,1,3456]{2,1,0:T(1,128)}), f32[8,1,3456]{2,1,0:T(1,128)S(1)}, u32[]{:S(2)}, u32[]{:S(2)}) async-start(f32[8,1,3456]{2,1,0:T(1,128)} %reshape.273), calls=%async_computation.8 | async-start | bytes 221184 | tf_op jit(solution)/shard_map/all_to_all | solution.py:148
  347.9 1.3 copy-start.6
